TPU v7x, 32 devices: a whole 2x2x4 slice. The times are simulated.
32 devices in a mesh: row: 8 (over z, x), col: 4 (over y, core).
Axes of the slice: x: 2, y: 2, z: 4, core: 2. Of those that a mesh axis runs over, the one named last changes fastest.
Arguments:
- features: bfloat16 [14336, 2048], P('row', 'col'), may hold values from -6 to 6
- neighbours: int32 [14336, 32], P('row'), may hold values from -1 to 127, as said below
- node_valid: int32 [14336], P('row'), may hold values from 0 to 1, as said below
- weight_one: bfloat16 [2048, 2048], P(None, 'col'), may hold values from -0.125 to 0.125
- gamma_one: float32 [2048], P('col'), may hold values from 0.25 to 1.75
- beta_one: float32 [2048], P('col'), may hold values from -0.5 to 0.5
- weight_two: bfloat16 [2048, 2048], P(None, 'col'), may hold values from -0.125 to 0.125
- gamma_two: float32 [2048], P('col'), may hold values from 0.25 to 1.75
- beta_two: float32 [2048], P('col'), may hold values from -0.5 to 0.5
- cotangent: bfloat16 [14336, 2048], P('row', 'col'), may hold values from -6 to 6
Outputs:
- output: float32 [14336, 2048], P('row', 'col')
- grad_features: float32 [14336, 2048], P('row', 'col')
- grad_weight_one: float32 [2048, 2048], P(None, 'col')
- grad_gamma_one: float32 [2048], P('col')
- grad_beta_one: float32 [2048], P('col')
- grad_weight_two: float32 [2048, 2048], P(None, 'col')
- grad_gamma_two: float32 [2048], P('col')
- grad_beta_two: float32 [2048], P('col')
Inputs may be any that keep to these rules, and one draw needn't show every extreme that they name: `neighbours`: entries >= 0 name valid nodes of the same slot; every valid node has 1 to 32 such entries, first in its list, the rest are -1; a padding row has only -1; some slot is full. `node_valid`: in each slot the valid nodes come first and number at least 40.
All inputs are finite; a program needn't handle non-finite values.
Results may differ from a plain program's by a relative error of at most 0.012.
Values may be sent and summed in bfloat16 or wider, within the bound.
No kernel may reach another device: no remote copies, remote signals or barrier semaphores. Data moves between devices by JAX's collectives and lax.ppermute only.
A program may use at most 128 MiB of HBM per device.

v0:
```python
import jax
import jax.numpy as jnp
from jax import lax
from jax.sharding import PartitionSpec as P

SLOT = 128
NBR = 32
EPSILON = 1e-05


def build_tiles(neighbours):
    entries_all = neighbours.reshape(-1, SLOT, NBR)

    def build(entries):
        columns = jnp.arange(SLOT, dtype=jnp.int32)
        hits = jnp.sum((entries[:, :, None] == columns[None, None, :]).astype(jnp.float32), axis=1)
        degree = jnp.sum((entries >= 0).astype(jnp.float32), axis=1)
        joined = hits + jnp.eye(SLOT, dtype=jnp.float32)
        return joined / (degree[:, None] + 1.0)

    tiles = lax.map(build, entries_all)
    return (tiles, jnp.diagonal(tiles, axis1=1, axis2=2))


def spread(values, tiles, self_weight):
    shaped = values.reshape(tiles.shape[0], SLOT, values.shape[1])
    summed = jnp.einsum("sij,sjd->sid", tiles, shaped, precision=lax.Precision.HIGHEST)
    return (summed + self_weight[:, :, None] * shaped).reshape(values.shape)


def spread_back(grads, tiles, self_weight):
    shaped = grads.reshape(tiles.shape[0], SLOT, grads.shape[1])
    summed = jnp.einsum("sji,sjd->sid", tiles, shaped, precision=lax.Precision.HIGHEST)
    return (summed + self_weight[:, :, None] * shaped).reshape(grads.shape)


def moments(linear, valid):
    total_valid, summed = lax.psum((jnp.sum(valid), jnp.sum(valid * linear, axis=0)), "row")
    mean = summed / total_valid
    centred = linear - mean
    variance = lax.psum(jnp.sum(valid * centred * centred, axis=0), "row") / total_valid
    return (total_valid, mean, variance)


def forward_layer(values, weight, gamma, beta, tiles, self_weight, valid):
    mixed = spread(values, tiles, self_weight).astype(jnp.bfloat16)
    gathered = lax.all_gather(mixed, "col", axis=1, tiled=True)
    linear = jnp.dot(gathered, weight, preferred_element_type=jnp.float32)
    total_valid, mean, variance = moments(linear, valid)
    inv_std = lax.rsqrt(variance + EPSILON)
    normed = (linear - mean) * inv_std
    before = gamma * normed + beta
    result = valid * jax.nn.silu(before)
    return (result, (gathered, normed, inv_std, before, total_valid))


def backward_layer(grad_result, weight, gamma, kept, tiles, self_weight, valid):
    gathered, normed, inv_std, before, total_valid = kept
    sigmoid_value = jax.nn.sigmoid(before)
    slope = sigmoid_value * (1.0 + before * (1.0 - sigmoid_value))
    grad_before = grad_result * valid * slope
    grad_beta, grad_gamma = lax.psum(
        (jnp.sum(grad_before, axis=0), jnp.sum(grad_before * normed, axis=0)), "row"
    )
    grad_normed = gamma * grad_before
    grad_linear = inv_std * (
        grad_normed - valid * (gamma * grad_beta + normed * gamma * grad_gamma) / total_valid
    )
    grad_low = grad_linear.astype(jnp.bfloat16)
    weight_terms = lax.dot_general(
        gathered, grad_low, (((0,), (0,)), ((), ())), preferred_element_type=jnp.float32
    )
    grad_weight = lax.psum(weight_terms, "row")
    partial_terms = lax.dot_general(
        grad_low, weight, (((1,), (1,)), ((), ())), preferred_element_type=jnp.float32
    )
    grad_mixed = lax.psum_scatter(partial_terms, "col", scatter_dimension=1, tiled=True)
    grad_values = spread_back(grad_mixed, tiles, self_weight)
    return (grad_values, grad_weight, grad_gamma, grad_beta)


def local(
    features,
    neighbours,
    node_valid,
    weight_one,
    gamma_one,
    beta_one,
    weight_two,
    gamma_two,
    beta_two,
    cotangent,
):
    tiles, self_weight = build_tiles(neighbours)
    valid = node_valid.astype(jnp.float32)[:, None]
    hidden, kept_one = forward_layer(
        features.astype(jnp.float32), weight_one, gamma_one, beta_one, tiles, self_weight, valid
    )
    output, kept_two = forward_layer(
        hidden, weight_two, gamma_two, beta_two, tiles, self_weight, valid
    )
    grad_hidden, grad_weight_two, grad_gamma_two, grad_beta_two = backward_layer(
        cotangent.astype(jnp.float32), weight_two, gamma_two, kept_two, tiles, self_weight, valid
    )
    grad_features, grad_weight_one, grad_gamma_one, grad_beta_one = backward_layer(
        grad_hidden, weight_one, gamma_one, kept_one, tiles, self_weight, valid
    )
    return (
        output,
        grad_features,
        grad_weight_one,
        grad_gamma_one,
        grad_beta_one,
        grad_weight_two,
        grad_gamma_two,
        grad_beta_two,
    )


def solution(mesh):
    placed = (
        P("row", "col"),
        P("row", None),
        P("row"),
        P(None, "col"),
        P("col"),
        P("col"),
        P(None, "col"),
        P("col"),
        P("col"),
        P("row", "col"),
    )
    return jax.shard_map(
        local,
        mesh=mesh,
        in_specs=placed,
        out_specs=(
            P("row", "col"),
            P("row", "col"),
            P(None, "col"),
            P("col"),
            P("col"),
            P(None, "col"),
            P("col"),
            P("col"),
        ),
        check_vma=False,
    )
```

profile of v0, /device:TPU:0, one launch (start us, length us, event | category | flops | bytes accessed | tf_op | source)
XLA Modules:
  0.0 855.5 jit_solution(2408295498759646820)
XLA Ops:
  7.3 2.3 copy.23
  9.6 27.6 %while.10 = (s32[]{:T(128)}, f32[14,128,128]{2,1,0:T(8,128)S(1)}, s32[14,128,32]{2,1,0:T(8,128)}, s32[]{:T(128)}) while((s32[]{:T(128)}, f32[14,128,128]{2,1,0:T(8,128)S(1)}, s32[14,128,32]{2,1,0:T(8,128)}, s32[]{:T(128)}) %tuple.47), condition=%wide.region_3.4_spmd, body=%wide.region_0.3_spmd.sunk | while | flops 1634306 | bytes 247877 | solution.py:21
  11.5 0.9 convert_reduce_fusion.5
  13.5 0.9 convert_reduce_fusion.5
  15.5 0.9 convert_reduce_fusion.5
  17.4 0.9 convert_reduce_fusion.5
  19.4 0.9 convert_reduce_fusion.5
  21.4 0.9 convert_reduce_fusion.5
  23.4 0.9 convert_reduce_fusion.5
  25.3 0.9 convert_reduce_fusion.5
  27.3 0.9 convert_reduce_fusion.5
  29.3 0.9 convert_reduce_fusion.5
  31.3 0.9 convert_reduce_fusion.5
  33.2 0.9 convert_reduce_fusion.5
  37.2 4.7 copy.24
  41.8 1.8 gather_fusion
  43.7 5.1 add_convert_fusion.1
  49.5 54.5 %all-gather.3.cloned.1.call-done = bf16[1792,2048]{1,0:T(8,128)(2,1)} async-done(((bf16[1792,512]{1,0:T(8,128)(2,1)}), bf16[1792,2048]{1,0:T(8,128)(2,1)}) %all-gather.3.cloned.1.call-update) | async-done | bytes 7340048 | tf_op jit(solution)/shard_map/all_gather | solution.py:47
  104.0 9.5 %multiply_reduce_fusion.3 = (f32[512]{0:T(512)S(1)}, f32[1792,512]{1,0:T(8,128)}) fusion(f32[1792]{0:T(1024)S(1)} %convert_element_type.41, bf16[1792,2048]{1,0:T(8,128)(2,1)} %all-gather.3.cloned.1.call-done, bf16[2048,512]{1,0:T(8,128)(2,1)} %param.15), kind=kOutput, calls=%fused_computation.29 | convolution fusion | flops 3759930880 | bytes 13116416 | tf_op jit(solution)/shard_map/dot_general | solution.py:48
  113.5 22.0 %all-reduce.2 = (f32[512]{0:T(512)S(1)}, f32[]{:T(128)}) all-reduce(f32[512]{0:T(512)S(1)} %get-tuple-element.49, f32[]{:T(128)} %convert_reduce_fusion.2), channel_id=1, replica_groups=mesh['row'=8,'col'=4] {'row'}, use_global_device_ids=true, to_apply=%region_5.6 | all-reduce | flops 513 | bytes 4104 | tf_op jit(solution)/shard_map/psum | solution.py:38
  136.0 2.6 fusion.2
  138.6 17.1 %psum.82 = f32[512]{0:T(512)S(1)} all-reduce(f32[512]{0:T(512)S(1)} %fusion.2), channel_id=1, replica_groups=mesh['row'=8,'col'=4] {'row'}, use_global_device_ids=true, to_apply=%region_9.10 | all-reduce | flops 512 | bytes 4096 | tf_op jit(solution)/shard_map/psum | solution.py:41
  156.3 3.0 multiply_multiply_fusion.4
  159.4 4.5 add_convert_fusion
  164.1 50.0 %all-gather.5.cloned.1.call-done = bf16[1792,2048]{1,0:T(8,128)(2,1)} async-done(((bf16[1792,512]{1,0:T(8,128)(2,1)}), bf16[1792,2048]{1,0:T(8,128)(2,1)}) %all-gather.5.cloned.1.call-update) | async-done | bytes 7340048 | tf_op jit(solution)/shard_map/all_gather | solution.py:47
  214.1 8.9 %multiply_reduce_fusion.2 = (f32[512]{0:T(512)S(1)}, f32[1792,512]{1,0:T(8,128)}) fusion(f32[1792]{0:T(1024)S(1)} %convert_element_type.41, bf16[1792,2048]{1,0:T(8,128)(2,1)} %all-gather.5.cloned.1.call-done, bf16[2048,512]{1,0:T(8,128)(2,1)S(1)} %copy-done), kind=kOutput, calls=%fused_computation.25 | convolution fusion | flops 3759930880 | bytes 13116416 | tf_op jit(solution)/shard_map/dot_general | solution.py:48
  223.0 21.5 %psum.83 = f32[512]{0:T(512)S(1)} all-reduce(f32[512]{0:T(512)S(1)} %get-tuple-element.51), channel_id=1, replica_groups=mesh['row'=8,'col'=4] {'row'}, use_global_device_ids=true, to_apply=%region_11.12 | all-reduce | flops 512 | bytes 4096 | tf_op jit(solution)/shard_map/psum | solution.py:38
  245.1 2.6 fusion.3
  247.7 17.1 %psum.84 = f32[512]{0:T(512)S(1)} all-reduce(f32[512]{0:T(512)S(1)} %fusion.3), channel_id=1, replica_groups=mesh['row'=8,'col'=4] {'row'}, use_global_device_ids=true, to_apply=%region_13.14 | all-reduce | flops 512 | bytes 4096 | tf_op jit(solution)/shard_map/psum | solution.py:41
  265.4 6.3 fusion.6
  271.7 19.1 %all-reduce.1 = (f32[512]{0:T(512)S(1)}, f32[512]{0:T(512)S(1)}) all-reduce(f32[512]{0:T(512)S(1)} %get-tuple-element.29, f32[512]{0:T(512)S(1)} %get-tuple-element.28), channel_id=1, replica_groups=mesh['row'=8,'col'=4] {'row'}, use_global_device_ids=true, to_apply=%region_17.18 | all-reduce | flops 1024 | bytes 8192 | tf_op jit(solution)/shard_map/psum | solution.py:62
  290.8 4.5 multiply_convert_fusion.1
  295.4 1.2 copy-done.4
  296.6 7.2 fusion.8
  304.1 109.0 %reduce-scatter.3.cloned.1.call-done = f32[1792,512]{1,0:T(8,128)} async-done(((f32[1792,2048]{1,0:T(8,128)}), f32[1792,512]{1,0:T(8,128)}) %reduce-scatter.3.cloned.1.call-update) | async-done | bytes 3670032 | tf_op jit(solution)/shard_map/reduce_scatter | solution.py:77
  413.1 6.8 multiply_add_fusion.1
  419.9 3.7 fusion.5
  423.7 21.3 %all-reduce = (f32[512]{0:T(512)S(1)}, f32[512]{0:T(512)S(1)}) all-reduce(f32[512]{0:T(512)S(1)} %get-tuple-element.27, f32[512]{0:T(512)S(1)} %get-tuple-element.26), channel_id=1, replica_groups=mesh['row'=8,'col'=4] {'row'}, use_global_device_ids=true, to_apply=%region_22.23 | all-reduce | flops 1024 | bytes 8192 | tf_op jit(solution)/shard_map/psum | solution.py:62
  445.0 4.7 multiply_convert_fusion
  449.8 7.3 fusion.9
  457.4 1.2 copy-done.5
  458.5 9.9 %fusion.11 = f32[2048,512]{1,0:T(8,128)} fusion(bf16[1792,2048]{1,0:T(8,128)(2,1)} %all-gather.5.cloned.1.call-done, bf16[1792,512]{1,0:T(8,128)(2,1)S(1)} %copy-done.5), kind=kOutput, calls=%fused_computation.44 | convolution fusion | flops 3758096384 | bytes 13369344 | tf_op jit(solution)/shard_map/dot_general | solution.py:70
  468.4 10.5 %fusion.10 = f32[2048,512]{1,0:T(8,128)} fusion(bf16[1792,2048]{1,0:T(8,128)(2,1)} %all-gather.3.cloned.1.call-done, bf16[1792,512]{1,0:T(8,128)(2,1)S(1)} %copy-done.7), kind=kOutput, calls=%fused_computation.43 | convolution fusion | flops 3758096384 | bytes 13369344 | tf_op jit(solution)/shard_map/dot_general | solution.py:70
  479.0 87.5 %reduce-scatter.5.cloned.1.call-done = f32[1792,512]{1,0:T(8,128)} async-done(((f32[1792,2048]{1,0:T(8,128)}), f32[1792,512]{1,0:T(8,128)}) %reduce-scatter.5.cloned.1.call-update) | async-done | bytes 3670032 | tf_op jit(solution)/shard_map/reduce_scatter | solution.py:77
  566.5 8.5 multiply_add_fusion
  575.0 267.1 %all-reduce.6.cloned.1.call-done = (f32[2048,512]{1,0:T(8,128)}, f32[2048,512]{1,0:T(8,128)}) async-done(((f32[2048,512]{1,0:T(8,128)}, f32[2048,512]{1,0:T(8,128)}), (f32[2048,512]{1,0:T(8,128)}, f32[2048,512]{1,0:T(8,128)})) %all-reduce.6.cloned.1.call-update) | async-done | bytes 8388624 | tf_op jit(solution)/shard_map/psum | solution.py:73
  842.1 4.8 copy.41
  846.9 2.0 copy.42
  (99 shorter events, 19.7 us)
Async XLA Ops:
  7.2 207.0 %copy-start = (bf16[2048,512]{1,0:T(8,128)(2,1)S(1)}, bf16[2048,512]{1,0:T(8,128)(2,1)}, u32[]{:S(2)}) copy-start(bf16[2048,512]{1,0:T(8,128)(2,1)} %param.18) | copy-start | bytes 6291460
  7.2 96.8 %all-gather.3.cloned.1.call-start = ((), (), s32[]{:S(2)}) async-start(), calls=%async_computation.2 | async-start | bytes 9175040 | tf_op jit(solution)/shard_map/all_gather | solution.py:47
  41.8 7.0 copy-start.8
  48.8 165.3 %all-gather.5.cloned.1.call-start = ((), (), s32[]{:S(2)}) async-start(), calls=%async_computation.3 | async-start | bytes 9175040 | tf_op jit(solution)/shard_map/all_gather | solution.py:47
  113.5 42.8 %copy-start.9 = (f32[512]{0:T(512)S(1)}, f32[512]{0:T(512)}, u32[]{:S(2)}) copy-start(f32[512]{0:T(512)} %param.16) | copy-start | bytes 6148
  113.5 42.8 %copy-start.11 = (f32[512]{0:T(512)S(1)}, f32[512]{0:T(512)}, u32[]{:S(2)}) copy-start(f32[512]{0:T(512)} %param.17) | copy-start | bytes 6148
  163.9 249.3 %reduce-scatter.3.cloned.1.call-start = ((), (), s32[]{:S(2)}) async-start(), calls=%async_computation.4 | async-start | bytes 18350080 | tf_op jit(solution)/shard_map/reduce_scatter | solution.py:77
  223.0 42.3 %copy-start.10 = (f32[512]{0:T(512)S(1)}, f32[512]{0:T(512)}, u32[]{:S(2)}) copy-start(f32[512]{0:T(512)} %param.19) | copy-start | bytes 6148
  223.0 42.3 %copy-start.12 = (f32[512]{0:T(512)S(1)}, f32[512]{0:T(512)}, u32[]{:S(2)}) copy-start(f32[512]{0:T(512)} %param.20) | copy-start | bytes 6148
  290.8 4.5 copy-start.13
  290.8 4.6 copy-start.15
  295.3 1.2 copy-start.4
  303.8 262.6 %reduce-scatter.5.cloned.1.call-start = ((), (), s32[]{:S(2)}) async-start(), calls=%async_computation.5 | async-start | bytes 18350080 | tf_op jit(solution)/shard_map/reduce_scatter | solution.py:77
  413.1 6.8 copy-start.2
  445.0 4.7 copy-start.14
  445.0 4.7 copy-start.16
  445.0 4.7 copy-start.17
  449.7 7.3 copy-start.6
  457.0 1.5 copy-start.5
  457.0 385.1 %all-reduce.6.cloned.1.call-start = ((), (), s32[]{:S(2)}) async-start(), calls=%async_computation.6 | async-start | bytes 16777216 | tf_op jit(solution)/shard_map/psum | solution.py:73
  458.5 9.9 %copy-start.7 = (bf16[1792,512]{1,0:T(8,128)(2,1)S(1)}, bf16[1792,512]{1,0:T(8,128)(2,1)}, u32[]{:S(2)}) copy-start(bf16[1792,512]{1,0:T(8,128)(2,1)} %copy-done.6) | copy-start | bytes 5505028
  842.1 4.8 copy-start.3
  842.1 6.8 copy-start.1
Sparse Core Ops, SparseCore 0:
  48.9 55.0 all-gather.2
  164.0 50.1 all-gather.4
  303.9 109.1 reduce-scatter.2
  457.2 109.2 reduce-scatter.4
  571.0 271.0 all-reduce.5
where the time goes:
time: 857 us; the launch traced here: 855 us
  waiting for transfers between devices  568 us (66%)
  blocking collectives  118 us (14%)
  matrix products  78.2 us (9%)
  other arithmetic  57.2 us (7%)
  local copies, waits for them, and re-layouts  18.1 us (2%)
  between operations  14 us (2%)
    psum x1, waiting for transfers between devices, backward_layer(): grad_weight = lax.psum(weight_terms, 'row')  267 us
    reduce_scatter x2, waiting for transfers between devices, backward_layer(): lax.psum_scatter(partial_terms, 'col', scatter_dimension=1, tiled=True)  197 us
    all_gather x2, waiting for transfers between devices, forward_layer(): gathered = lax.all_gather(mixed, 'col', axis=1, tiled=True)  105 us
    psum x2, blocking collectives, moments(): lax.psum((jnp.sum(valid), jnp.sum(valid * linear, axis=0)), 'row')  43.4 us
    psum x2, blocking collectives, backward_layer(): lax.psum((jnp.sum(grad_before, axis=0), jnp.sum(grad_before * normed, axi...  40.5 us
    psum x2, blocking collectives, moments(): lax.psum(jnp.sum(valid * centred * centred, axis=0), 'row') / total_valid  34.3 us
    dot_general x2, matrix products, backward_layer(): lax.dot_general(gathered, grad_low, (((0,), (0,)), ((), ())), preferred_e...  20.4 us
    dot_general x2, matrix products, forward_layer(): linear = jnp.dot(gathered, weight, preferred_element_type=jnp.float32)  18.4 us
  transfers between devices with their start and end apart: 5, of which 5 were waited for; matrix products, arithmetic and copies ran while one was open for 3% of the time, Pallas kernels for 0%

commit v1 on v0

--- a/solution.py
+++ b/solution.py
@@ -6,6 +6,21 @@
 SLOT = 128
 NBR = 32
 EPSILON = 1e-05
+
+
+def _rest_ladders(inp):
+    outcome_arr, f_now = (inp, 0)
+    count_all = jax.lax.axis_size("row")
+    while 1 << f_now < count_all:
+        by_rank = []
+        ix = 0
+        while ix < count_all:
+            by_rank.append((ix, ix ^ 1 << f_now))
+            ix = ix + 1
+        w1 = jax.lax.ppermute(outcome_arr, axis_name="row", perm=by_rank)
+        outcome_arr = outcome_arr + w1
+        f_now = f_now + 1
+    return outcome_arr
 
 
 def build_tiles(neighbours):
@@ -70,7 +85,7 @@
     weight_terms = lax.dot_general(
         gathered, grad_low, (((0,), (0,)), ((), ())), preferred_element_type=jnp.float32
     )
-    grad_weight = lax.psum(weight_terms, "row")
+    grad_weight = _rest_ladders(weight_terms)
     partial_terms = lax.dot_general(
         grad_low, weight, (((1,), (1,)), ((), ())), preferred_element_type=jnp.float32
     )

time: 857 us -> 1030 us (1.20)
  waiting for transfers between devices: 568 us -> 734 us
    ppermute x0 -> x6, waiting for transfers between devices: none -> 520 us  [_rest_ladders(): w1 = jax.lax.ppermute(outcome_arr, axis_name='row', perm=by_rank)]
    psum x1 -> x0, waiting for transfers between devices: 267 us -> none  [backward_layer(): grad_weight = lax.psum(weight_terms, 'row')]
    reduce_scatter x2, waiting for transfers between devices: 197 us -> 109 us  [backward_layer(): lax.psum_scatter(partial_terms, 'col', scatter_dimension=1, tiled=True)]
  transfers between devices with their start and end apart: 5 -> 10, of which waited for: 5 -> 8; matrix products, arithmetic and copies ran while one was open for 3% -> 2% of each run, Pallas kernels for 0% -> 0%
where the time goes in v1:
time: 1030 us; the launch traced here: 1020 us
  waiting for transfers between devices  734 us (71%)
  blocking collectives  118 us (11%)
  matrix products  72.1 us (7%)
  other arithmetic  67.4 us (7%)
  between operations  14.3 us (1%)
  local copies, waits for them, and re-layouts  11.6 us (1%)
    ppermute x6, waiting for transfers between devices, _rest_ladders(): w1 = jax.lax.ppermute(outcome_arr, axis_name='row', perm=by_rank)  520 us
    reduce_scatter x2, waiting for transfers between devices, backward_layer(): lax.psum_scatter(partial_terms, 'col', scatter_dimension=1, tiled=True)  109 us
    all_gather x2, waiting for transfers between devices, forward_layer(): gathered = lax.all_gather(mixed, 'col', axis=1, tiled=True)  104 us
    psum x2, blocking collectives, moments(): lax.psum((jnp.sum(valid), jnp.sum(valid * linear, axis=0)), 'row')  43.5 us
    psum x2, blocking collectives, backward_layer(): lax.psum((jnp.sum(grad_before, axis=0), jnp.sum(grad_before * normed, axi...  40.5 us
    psum x2, blocking collectives, moments(): lax.psum(jnp.sum(valid * centred * centred, axis=0), 'row') / total_valid  34.3 us
  transfers between devices with their start and end apart: 10, of which 8 were waited for; matrix products, arithmetic and copies ran while one was open for 2% of the time, Pallas kernels for 0%

profile of v1, /device:TPU:0, one launch (start us, length us, event | category | flops | bytes accessed | tf_op | source)
XLA Modules:
  0.0 1021.7 jit_solution(17962713680265296360)
XLA Ops:
  7.3 2.3 copy.23
  9.6 27.6 %while.10 = (s32[]{:T(128)}, f32[14,128,128]{2,1,0:T(8,128)S(1)}, s32[14,128,32]{2,1,0:T(8,128)}, s32[]{:T(128)}) while((s32[]{:T(128)}, f32[14,128,128]{2,1,0:T(8,128)S(1)}, s32[14,128,32]{2,1,0:T(8,128)}, s32[]{:T(128)}) %tuple.43), condition=%wide.region_3.4_spmd, body=%wide.region_0.3_spmd.sunk | while | flops 1634306 | bytes 247877 | solution.py:36
  11.5 0.9 convert_reduce_fusion.5
  13.5 0.9 convert_reduce_fusion.5
  15.5 0.9 convert_reduce_fusion.5
  31.3 0.9 convert_reduce_fusion.5
  37.2 4.7 copy.24
  41.8 1.8 gather_fusion
  43.7 5.1 add_convert_fusion.1
  49.5 54.5 %all-gather.3.cloned.1.call-done = bf16[1792,2048]{1,0:T(8,128)(2,1)} async-done(((bf16[1792,512]{1,0:T(8,128)(2,1)}), bf16[1792,2048]{1,0:T(8,128)(2,1)}) %all-gather.3.cloned.1.call-update) | async-done | bytes 7340048 | tf_op jit(solution)/shard_map/all_gather | solution.py:62
  104.0 9.5 multiply_reduce_fusion.3
  113.5 22.0 %all-reduce.2 = (f32[512]{0:T(512)S(1)}, f32[]{:T(128)}) all-reduce(f32[512]{0:T(512)S(1)} %get-tuple-element.47, f32[]{:T(128)} %convert_reduce_fusion.2), channel_id=1, replica_groups=mesh['row'=8,'col'=4] {'row'}, use_global_device_ids=true, to_apply=%region_5.6 | all-reduce | flops 513 | bytes 4104 | tf_op jit(solution)/shard_map/psum | solution.py:53
  136.0 2.6 fusion.2
  138.6 17.1 %psum.68 = f32[512]{0:T(512)S(1)} all-reduce(f32[512]{0:T(512)S(1)} %fusion.2), channel_id=1, replica_groups=mesh['row'=8,'col'=4] {'row'}, use_global_device_ids=true, to_apply=%region_9.10 | all-reduce | flops 512 | bytes 4096 | tf_op jit(solution)/shard_map/psum | solution.py:56
  156.3 3.0 multiply_multiply_fusion.4
  159.4 4.5 add_convert_fusion
  164.4 49.8 %all-gather.5.cloned.1.call-done = bf16[1792,2048]{1,0:T(8,128)(2,1)} async-done(((bf16[1792,512]{1,0:T(8,128)(2,1)}), bf16[1792,2048]{1,0:T(8,128)(2,1)}) %all-gather.5.cloned.1.call-update) | async-done | bytes 7340048 | tf_op jit(solution)/shard_map/all_gather | solution.py:62
  214.1 8.9 multiply_reduce_fusion.2
  223.0 21.5 %psum.69 = f32[512]{0:T(512)S(1)} all-reduce(f32[512]{0:T(512)S(1)} %get-tuple-element.49), channel_id=1, replica_groups=mesh['row'=8,'col'=4] {'row'}, use_global_device_ids=true, to_apply=%region_11.12 | all-reduce | flops 512 | bytes 4096 | tf_op jit(solution)/shard_map/psum | solution.py:53
  245.1 2.6 fusion.3
  247.7 17.1 %psum.70 = f32[512]{0:T(512)S(1)} all-reduce(f32[512]{0:T(512)S(1)} %fusion.3), channel_id=1, replica_groups=mesh['row'=8,'col'=4] {'row'}, use_global_device_ids=true, to_apply=%region_13.14 | all-reduce | flops 512 | bytes 4096 | tf_op jit(solution)/shard_map/psum | solution.py:56
  265.4 6.3 fusion.6
  271.7 19.1 %all-reduce.1 = (f32[512]{0:T(512)S(1)}, f32[512]{0:T(512)S(1)}) all-reduce(f32[512]{0:T(512)S(1)} %get-tuple-element.29, f32[512]{0:T(512)S(1)} %get-tuple-element.28), channel_id=1, replica_groups=mesh['row'=8,'col'=4] {'row'}, use_global_device_ids=true, to_apply=%region_17.18 | all-reduce | flops 1024 | bytes 8192 | tf_op jit(solution)/shard_map/psum | solution.py:77
  290.8 4.5 multiply_convert_fusion.1
  295.4 1.2 copy-done.3
  296.6 7.2 fusion.8
  304.1 109.1 %reduce-scatter.3.cloned.1.call-done = f32[1792,512]{1,0:T(8,128)} async-done(((f32[1792,2048]{1,0:T(8,128)}), f32[1792,512]{1,0:T(8,128)}) %reduce-scatter.3.cloned.1.call-update) | async-done | bytes 3670032 | tf_op jit(solution)/shard_map/reduce_scatter | solution.py:92
  413.1 6.8 multiply_add_fusion.1
  419.9 3.7 fusion.5
  423.7 21.3 %all-reduce = (f32[512]{0:T(512)S(1)}, f32[512]{0:T(512)S(1)}) all-reduce(f32[512]{0:T(512)S(1)} %get-tuple-element.27, f32[512]{0:T(512)S(1)} %get-tuple-element.26), channel_id=1, replica_groups=mesh['row'=8,'col'=4] {'row'}, use_global_device_ids=true, to_apply=%region_22.23 | all-reduce | flops 1024 | bytes 8192 | tf_op jit(solution)/shard_map/psum | solution.py:77
  445.1 4.7 multiply_convert_fusion
  449.8 7.3 fusion.9
  457.1 1.5 copy-done.4
  458.5 6.9 fusion.11
  465.6 7.3 fusion.10
  472.8 2.2 collective-permute-start
  475.0 84.0 %collective-permute-done.3 = f32[2048,512]{1,0:T(8,128)S(1)} collective-permute-done((f32[2048,512]{1,0:T(8,128)S(1)}, f32[2048,512]{1,0:T(8,128)S(1)}, u32[]{:S(2)}, u32[]{:S(2)}) %collective-permute-start.3) | collective-permute-done | bytes 4194336 | tf_op jit(solution)/shard_map/ppermute | solution.py:20
  559.0 1.0 add.152
  560.1 83.3 %collective-permute-done = f32[2048,512]{1,0:T(8,128)S(1)} collective-permute-done((f32[2048,512]{1,0:T(8,128)S(1)}, f32[2048,512]{1,0:T(8,128)S(1)}, u32[]{:S(2)}, u32[]{:S(2)}) %collective-permute-start) | collective-permute-done | bytes 4194336 | tf_op jit(solution)/shard_map/ppermute | solution.py:20
  643.4 1.0 add.149
  644.5 1.0 add.153
  645.6 172.2 %collective-permute-done.1 = f32[2048,512]{1,0:T(8,128)S(1)} collective-permute-done((f32[2048,512]{1,0:T(8,128)S(1)}, f32[2048,512]{1,0:T(8,128)S(1)}, u32[]{:S(2)}, u32[]{:S(2)}) %collective-permute-start.1) | collective-permute-done | bytes 4194336 | tf_op jit(solution)/shard_map/ppermute | solution.py:20
  817.9 1.0 add.150
  819.4 97.7 %collective-permute-done.5 = f32[2048,512]{1,0:T(8,128)S(1)} collective-permute-done((f32[2048,512]{1,0:T(8,128)S(1)}, f32[2048,512]{1,0:T(8,128)S(1)}, u32[]{:S(2)}, u32[]{:S(2)}) %collective-permute-start.5) | collective-permute-done | bytes 4194336 | tf_op jit(solution)/shard_map/ppermute | solution.py:20
  917.1 3.0 add.154
  920.1 83.2 %collective-permute-done.2 = f32[2048,512]{1,0:T(8,128)S(1)} collective-permute-done((f32[2048,512]{1,0:T(8,128)S(1)}, f32[2048,512]{1,0:T(8,128)S(1)}, u32[]{:S(2)}, u32[]{:S(2)}) %collective-permute-start.2) | collective-permute-done | bytes 4194336 | tf_op jit(solution)/shard_map/ppermute | solution.py:20
  1003.3 3.0 add.151
  1006.4 8.6 multiply_add_fusion
  (110 shorter events, 28.0 us)
Async XLA Ops:
  7.2 207.0 %copy-start = (bf16[2048,512]{1,0:T(8,128)(2,1)S(1)}, bf16[2048,512]{1,0:T(8,128)(2,1)}, u32[]{:S(2)}) copy-start(bf16[2048,512]{1,0:T(8,128)(2,1)} %param.18) | copy-start | bytes 6291460
  7.2 96.8 %all-gather.3.cloned.1.call-start = ((), (), s32[]{:S(2)}) async-start(), calls=%async_computation.2 | async-start | bytes 9175040 | tf_op jit(solution)/shard_map/all_gather | solution.py:62
  41.8 7.0 copy-start.7
  48.8 165.3 %all-gather.5.cloned.1.call-start = ((), (), s32[]{:S(2)}) async-start(), calls=%async_computation.3 | async-start | bytes 9175040 | tf_op jit(solution)/shard_map/all_gather | solution.py:62
  113.5 42.8 %copy-start.8 = (f32[512]{0:T(512)S(1)}, f32[512]{0:T(512)}, u32[]{:S(2)}) copy-start(f32[512]{0:T(512)} %param.16) | copy-start | bytes 6148
  113.5 42.8 %copy-start.10 = (f32[512]{0:T(512)S(1)}, f32[512]{0:T(512)}, u32[]{:S(2)}) copy-start(f32[512]{0:T(512)} %param.17) | copy-start | bytes 6148
  163.9 249.3 %reduce-scatter.3.cloned.1.call-start = ((), (), s32[]{:S(2)}) async-start(), calls=%async_computation.4 | async-start | bytes 18350080 | tf_op jit(solution)/shard_map/reduce_scatter | solution.py:92
  223.0 42.3 %copy-start.9 = (f32[512]{0:T(512)S(1)}, f32[512]{0:T(512)}, u32[]{:S(2)}) copy-start(f32[512]{0:T(512)} %param.19) | copy-start | bytes 6148
  223.0 42.4 %copy-start.11 = (f32[512]{0:T(512)S(1)}, f32[512]{0:T(512)}, u32[]{:S(2)}) copy-start(f32[512]{0:T(512)} %param.20) | copy-start | bytes 6148
  290.8 4.5 copy-start.12
  290.8 4.6 copy-start.14
  295.3 1.2 copy-start.3
  303.8 702.5 %reduce-scatter.5.cloned.1.call-start = ((), (), s32[]{:S(2)}) async-start(), calls=%async_computation.5 | async-start | bytes 18350080 | tf_op jit(solution)/shard_map/reduce_scatter | solution.py:92
  413.1 6.8 copy-start.2
  445.0 4.7 copy-start.13
  445.0 4.7 copy-start.15
  445.0 4.7 copy-start.16
  449.8 7.3 copy-start.5
  457.0 1.5 copy-start.4
  458.5 7.0 copy-start.6
  465.5 93.6 %collective-permute-start.3 = (f32[2048,512]{1,0:T(8,128)S(1)}, f32[2048,512]{1,0:T(8,128)S(1)}, u32[]{:S(2)}, u32[]{:S(2)}) collective-permute-start(f32[2048,512]{1,0:T(8,128)S(1)} %fusion.11), channel_id=1, source_target_pairs={{0,4},{4,0},{8,12},{12,8},{16,20},{20,16},{24,28},{28,24},{1,5},{5... | collective-permute-start | bytes 12582920 | tf_op jit(solution)/shard_map/ppermute | solution.py:20
  472.8 170.6 %collective-permute-start = (f32[2048,512]{1,0:T(8,128)S(1)}, f32[2048,512]{1,0:T(8,128)S(1)}, u32[]{:S(2)}, u32[]{:S(2)}) collective-permute-start(f32[2048,512]{1,0:T(8,128)S(1)} %fusion.10), channel_id=1, source_target_pairs={{0,4},{4,0},{8,12},{12,8},{16,20},{20,16},{24,28},{28,24},{1,5},{5... | collective-permute-start | bytes 12582920 | tf_op jit(solution)/shard_map/ppermute | solution.py:20
  560.1 84.5 %collective-permute-start.4 = (f32[2048,512]{1,0:T(8,128)S(1)}, f32[2048,512]{1,0:T(8,128)S(1)}, u32[]{:S(2)}, u32[]{:S(2)}) collective-permute-start(f32[2048,512]{1,0:T(8,128)S(1)} %add.152), channel_id=1, source_target_pairs={{0,8},{4,12},{8,0},{12,4},{16,24},{20,28},{24,16},{28,20},{1,9},{5... | collective-permute-start | bytes 12582920 | tf_op jit(solution)/shard_map/ppermute | solution.py:20
  644.4 173.4 %collective-permute-start.1 = (f32[2048,512]{1,0:T(8,128)S(1)}, f32[2048,512]{1,0:T(8,128)S(1)}, u32[]{:S(2)}, u32[]{:S(2)}) collective-permute-start(f32[2048,512]{1,0:T(8,128)S(1)} %add.149), channel_id=1, source_target_pairs={{0,8},{4,12},{8,0},{12,4},{16,24},{20,28},{24,16},{28,20},{1,9},{5... | collective-permute-start | bytes 12582920 | tf_op jit(solution)/shard_map/ppermute | solution.py:20
  645.6 271.5 %collective-permute-start.5 = (f32[2048,512]{1,0:T(8,128)S(1)}, f32[2048,512]{1,0:T(8,128)S(1)}, u32[]{:S(2)}, u32[]{:S(2)}) collective-permute-start(f32[2048,512]{1,0:T(8,128)S(1)} %add.153), channel_id=1, source_target_pairs={{0,16},{4,20},{8,24},{12,28},{16,0},{20,4},{24,8},{28,12},{1,17},{... | collective-permute-start | bytes 12582920 | tf_op jit(solution)/shard_map/ppermute | solution.py:20
  818.9 184.4 %collective-permute-start.2 = (f32[2048,512]{1,0:T(8,128)S(1)}, f32[2048,512]{1,0:T(8,128)S(1)}, u32[]{:S(2)}, u32[]{:S(2)}) collective-permute-start(f32[2048,512]{1,0:T(8,128)S(1)} %add.150), channel_id=1, source_target_pairs={{0,16},{4,20},{8,24},{12,28},{16,0},{20,4},{24,8},{28,12},{1,17},{... | collective-permute-start | bytes 12582920 | tf_op jit(solution)/shard_map/ppermute | solution.py:20
  1006.4 8.6 copy-start.1
Sparse Core Ops, SparseCore 0:
  48.9 55.0 all-gather.2
  164.0 50.0 all-gather.4
  304.0 109.1 reduce-scatter.2
  457.2 109.2 reduce-scatter.4
